TPU v7x, 32 devices: a whole 2x2x4 slice. The times are simulated.
32 devices in a mesh: gx: 8 (over y, x, core), gy: 4 (over z).
Axes of the slice: x: 2, y: 2, z: 4, core: 2. Of those that a mesh axis runs over, the one named last changes fastest.
Arguments:
- probe_signs: int32 [32, 16, 64, 128], P(None, 'gx', 'gy'), may hold values from 0 to 1
- diagonal: float32 [16, 64, 128], P('gx', 'gy'), may hold values from 0.25 to 4
Outputs:
- diagonal_blocks: float32 [3, 32, 32], replicated
- offdiag_blocks: float32 [3, 32, 32], replicated
- next_block: float32 [32, 16, 64, 128], P(None, 'gx', 'gy')
All inputs are finite; a program needn't handle non-finite values.
Results may differ from a plain program's by a relative error of at most 0.0006.
Values sent between devices are 32-bit elements; how exact they have to be, the bound alone decides.
A program may use at most 64 MiB of HBM per device.

v0:
```python
import jax
import jax.numpy as jnp
from jax import lax
from jax.sharding import PartitionSpec as P

ITERS = 3


def with_halo(block, sides, width):
    for axis, dim in sides:
        count = lax.axis_size(axis)
        forward = [(i, i + 1) for i in range(count - 1)]
        forward.append((count - 1, 0))
        backward = [(target, source) for source, target in forward]
        low = lax.ppermute(
            lax.slice_in_dim(block, block.shape[dim] - width, None, axis=dim), axis, forward
        )
        high = lax.ppermute(lax.slice_in_dim(block, 0, width, axis=dim), axis, backward)
        block = jnp.concatenate([low, block, high], axis=dim)
    return block


def stencil(vectors, diagonal):
    padded = with_halo(vectors, (("gx", 1), ("gy", 2)), 1)
    beside = padded[:, 2:, 1:-1] + padded[:, :-2, 1:-1] + padded[:, 1:-1, 2:] + padded[:, 1:-1, :-2]
    beside = beside + jnp.roll(vectors, 1, 3) + jnp.roll(vectors, -1, 3)
    return (6.0 + diagonal)[None] * vectors - beside


def inner_block(left, right):
    return jnp.einsum("pxyz,qxyz->pq", left, right, precision=lax.Precision.HIGHEST)


def combine(vectors, matrix):
    return jnp.einsum("pxyz,pq->qxyz", vectors, matrix, precision=lax.Precision.HIGHEST)


def small_product(left, right):
    return jnp.dot(left, right, precision=lax.Precision.HIGHEST)


def inverse_lower(gram_matrix):
    lower_factor = jnp.linalg.cholesky(gram_matrix)
    identity_matrix = jnp.eye(gram_matrix.shape[0], dtype=gram_matrix.dtype)
    inverse = lax.linalg.triangular_solve(lower_factor, identity_matrix, left_side=True, lower=True)
    return (lower_factor, inverse)


def per_device(probe_signs, diagonal):
    total_cells = (
        probe_signs.shape[1]
        * lax.axis_size("gx")
        * probe_signs.shape[2]
        * lax.axis_size("gy")
        * probe_signs.shape[3]
    )
    scale_factor = 1.0 / jnp.sqrt(jnp.float32(total_cells))
    probes = (2.0 * probe_signs.astype(jnp.float32) - 1.0) * scale_factor
    probe_matrix = lax.psum(inner_block(probes, probes), ("gx", "gy"))
    lower_factor, inverse = inverse_lower(probe_matrix)
    current = combine(probes, inverse.T)
    previous = None
    coupling = None
    alphas = []
    betas = []
    for iteration in range(ITERS):
        image = stencil(current, diagonal)
        if previous is not None:
            image = image - combine(previous, coupling)
        projected, image_gram = lax.psum(
            (inner_block(current, image), inner_block(image, image)), ("gx", "gy")
        )
        remain = image - combine(current, projected)
        remain_gram = image_gram - small_product(projected.T, projected)
        lower_factor, inverse = inverse_lower(remain_gram)
        alphas.append(projected)
        betas.append(lower_factor.T)
        previous = current
        coupling = lower_factor
        current = combine(remain, inverse.T)
    return (jnp.stack(alphas), jnp.stack(betas), current)


def solution(mesh):
    in_specs = (P(None, "gx", "gy", None), P("gx", "gy", None))
    out_specs = (P(), P(), P(None, "gx", "gy", None))
    return jax.shard_map(
        per_device, mesh=mesh, in_specs=in_specs, out_specs=out_specs, check_vma=False
    )
```

profile of v0, /device:TPU:14, one launch (start us, length us, event | category | flops | bytes accessed | tf_op | source)
XLA Modules:
  0.0 253.6 jit_solution(12887706050572880338)
XLA Ops:
  0.6 1.1 add_multiply_fusion
  1.8 0.8 convolution_bitcast_fusion.10
  2.6 40.3 %psum.49 = f32[32,32]{0,1:T(8,128)S(1)} all-reduce(f32[32,32]{0,1:T(8,128)S(1)} %convolution_bitcast_fusion.10), channel_id=1, replica_groups=mesh['gx'=8,'gy'=4] {'gx','gy'}, use_global_device_ids=true, to_apply=%region_0.0 | all-reduce | flops 1024 | bytes 8192 | tf_op jit(solution)/shard_map/psum | solution.py:59
  43.0 2.9 %cholesky.74 = f32[32,32]{1,0:T(8,128)S(1)} custom-call(f32[32,32]{1,0:T(8,128)S(1)} %fusion.38), custom_call_target="Cholesky" | custom-call | tf_op jit(solution)/shard_map/jit(cholesky)/cholesky | solution.py:43
  47.3 2.4 custom-call.8
  49.9 0.9 fusion.18
  50.9 1.7 collective-permute-start
  53.1 3.7 %collective-permute-done.1 = f32[32,1,16,128]{3,0,2,1:T(8,128)S(1)} collective-permute-done((f32[32,1,16,128]{3,0,2,1:T(8,128)S(1)}, f32[32,1,16,128]{3,0,2,1:T(8,128)S(1)}, u32[]{:S(2)}, u32[]{:S(2)}) %collective-permute-start.1) | collective-permute-done | bytes 262176 | tf_op jit(solution)/shard_map/ppermute | solution.py:15
  56.8 0.9 collective-permute-done
  58.3 1.5 collective-permute-start.3
  59.8 2.2 collective-permute-done.2
  62.0 1.4 collective-permute-done.3
  65.0 44.6 %all-reduce.2 = (f32[32,32]{0,1:T(8,128)S(1)}, f32[32,32]{1,0:T(8,128)S(1)}) all-reduce(f32[32,32]{0,1:T(8,128)S(1)} %convolution_bitcast_fusion.7, f32[32,32]{1,0:T(8,128)S(1)} %convolution_bitcast_fusion.8), channel_id=1, replica_groups=mesh['gx'=8,'gy'=4] {'gx','gy'}, use_global_device_ids=true, to_apply=%region_4.7 | all-reduce | flops 2048 | bytes 16384 | tf_op jit(solution)/shard_map/psum | solution.py:70
  110.5 2.9 %cholesky.85 = f32[32,32]{1,0:T(8,128)S(1)} custom-call(f32[32,32]{1,0:T(8,128)S(1)} %fusion.36), custom_call_target="Cholesky" | custom-call | tf_op jit(solution)/shard_map/jit(cholesky)/cholesky | solution.py:43
  114.8 2.4 custom-call.9
  118.2 1.7 collective-permute-start.4
  120.1 5.4 %collective-permute-done.5 = f32[32,1,16,128]{3,0,2,1:T(8,128)S(1)} collective-permute-done((f32[32,1,16,128]{3,0,2,1:T(8,128)S(1)}, f32[32,1,16,128]{3,0,2,1:T(8,128)S(1)}, u32[]{:S(2)}, u32[]{:S(2)}) %collective-permute-start.5) | collective-permute-done | bytes 262176 | tf_op jit(solution)/shard_map/ppermute | solution.py:15
  125.6 2.0 collective-permute-start.7
  127.8 2.2 collective-permute-done.6
  130.9 1.6 convolution_subtract_fusion.3
  133.6 42.3 %all-reduce.1 = (f32[32,32]{0,1:T(8,128)S(1)}, f32[32,32]{1,0:T(8,128)S(1)}) all-reduce(f32[32,32]{0,1:T(8,128)S(1)} %convolution_bitcast_fusion.4, f32[32,32]{1,0:T(8,128)S(1)} %convolution_bitcast_fusion.5), channel_id=1, replica_groups=mesh['gx'=8,'gy'=4] {'gx','gy'}, use_global_device_ids=true, to_apply=%region_6.9 | all-reduce | flops 2048 | bytes 16384 | tf_op jit(solution)/shard_map/psum | solution.py:70
  176.8 2.9 %cholesky.96 = f32[32,32]{1,0:T(8,128)S(1)} custom-call(f32[32,32]{1,0:T(8,128)S(1)} %fusion.33), custom_call_target="Cholesky" | custom-call | tf_op jit(solution)/shard_map/jit(cholesky)/cholesky | solution.py:43
  181.1 2.4 custom-call.10
  184.4 1.7 collective-permute-start.8
  186.4 4.8 %collective-permute-done.9 = f32[32,1,16,128]{3,0,2,1:T(8,128)S(1)} collective-permute-done((f32[32,1,16,128]{3,0,2,1:T(8,128)S(1)}, f32[32,1,16,128]{3,0,2,1:T(8,128)S(1)}, u32[]{:S(2)}, u32[]{:S(2)}) %collective-permute-start.9) | collective-permute-done | bytes 262176 | tf_op jit(solution)/shard_map/ppermute | solution.py:15
  191.3 2.0 collective-permute-start.11
  193.5 2.0 collective-permute-done.10
  196.1 1.6 convolution_subtract_fusion.1
  198.7 44.0 %all-reduce = (f32[32,32]{1,0:T(8,128)S(1)}, f32[32,32]{0,1:T(8,128)S(1)}) all-reduce(f32[32,32]{1,0:T(8,128)S(1)} %convolution_bitcast_fusion.2, f32[32,32]{0,1:T(8,128)S(1)} %convolution_bitcast_fusion.1), channel_id=1, replica_groups=mesh['gx'=8,'gy'=4] {'gx','gy'}, use_global_device_ids=true, to_apply=%region_7.10 | all-reduce | flops 2048 | bytes 16384 | tf_op jit(solution)/shard_map/psum | solution.py:70
  243.6 2.9 %cholesky.107 = f32[32,32]{1,0:T(8,128)S(1)} custom-call(f32[32,32]{1,0:T(8,128)S(1)} %fusion.30), custom_call_target="Cholesky" | custom-call | tf_op jit(solution)/shard_map/jit(cholesky)/cholesky | solution.py:43
  247.9 2.4 custom-call.11
  251.2 1.1 copy.22
  (68 shorter events, 19.4 us)
Async XLA Ops:
  50.9 6.0 %collective-permute-start.1 = (f32[32,1,16,128]{3,0,2,1:T(8,128)S(1)}, f32[32,1,16,128]{3,0,2,1:T(8,128)S(1)}, u32[]{:S(2)}, u32[]{:S(2)}) collective-permute-start(f32[32,1,16,128]{3,0,2,1:T(8,128)S(1)} %get-tuple-element.36), channel_id=1, source_target_pairs={{0,4},{4,8},{8,12},{12,16},{16,20},{20,24},{24,28},{28,0},{1,5},{5... | collective-permute-start | bytes 786440 | tf_op jit(solution)/shard_map/ppermute | solution.py:15
  50.9 6.8 %collective-permute-start = (f32[32,1,16,128]{3,0,2,1:T(8,128)S(1)}, f32[32,1,16,128]{3,0,2,1:T(8,128)S(1)}, u32[]{:S(2)}, u32[]{:S(2)}) collective-permute-start(f32[32,1,16,128]{3,0,2,1:T(8,128)S(1)} %get-tuple-element.37), channel_id=1, source_target_pairs={{4,0},{8,4},{12,8},{16,12},{20,16},{24,20},{28,24},{0,28},{5,1},{9... | collective-permute-start | bytes 786440 | tf_op jit(solution)/shard_map/ppermute | solution.py:18
  53.1 6.7 %copy-start = (f32[2,16,128]{2,1,0:T(8,128)S(1)}, f32[2,16,128]{2,1,0:T(8,128)}, u32[]{:S(2)}) copy-start(f32[2,16,128]{2,1,0:T(8,128)} %param.6) | copy-start | bytes 49156
  57.7 4.3 %collective-permute-start.2 = (f32[32,4,1,128]{3,0,2,1:T(8,128)S(1)}, f32[32,4,1,128]{3,0,2,1:T(8,128)S(1)}, u32[]{:S(2)}, u32[]{:S(2)}) collective-permute-start(f32[32,4,1,128]{3,0,2,1:T(8,128)S(1)} %get-tuple-element.18), channel_id=1, source_target_pairs={{1,0},{2,1},{3,2},{0,3},{5,4},{6,5},{7,6},{4,7},{9,8},{10,9},{11,1... | collective-permute-start | bytes 196616 | tf_op jit(solution)/shard_map/ppermute | solution.py:18
  58.3 5.1 %collective-permute-start.3 = (f32[32,4,1,128]{3,0,2,1:T(8,128)S(1)}, f32[32,4,1,128]{3,0,2,1:T(8,128)S(1)}, u32[]{:S(2)}, u32[]{:S(2)}) collective-permute-start(f32[32,4,1,128]{3,0,2,1:T(8,128)S(1)} %get-tuple-element.19), channel_id=1, source_target_pairs={{0,1},{1,2},{2,3},{3,0},{4,5},{5,6},{6,7},{7,4},{8,9},{9,10},{10,1... | collective-permute-start | bytes 196616 | tf_op jit(solution)/shard_map/ppermute | solution.py:15
  118.1 7.4 %collective-permute-start.5 = (f32[32,1,16,128]{3,0,2,1:T(8,128)S(1)}, f32[32,1,16,128]{3,0,2,1:T(8,128)S(1)}, u32[]{:S(2)}, u32[]{:S(2)}) collective-permute-start(f32[32,1,16,128]{3,0,2,1:T(8,128)S(1)} %get-tuple-element.30), channel_id=1, source_target_pairs={{0,4},{4,8},{8,12},{12,16},{16,20},{20,24},{24,28},{28,0},{1,5},{5... | collective-permute-start | bytes 786440 | tf_op jit(solution)/shard_map/ppermute | solution.py:15
  118.2 7.4 %collective-permute-start.4 = (f32[32,1,16,128]{3,0,2,1:T(8,128)S(1)}, f32[32,1,16,128]{3,0,2,1:T(8,128)S(1)}, u32[]{:S(2)}, u32[]{:S(2)}) collective-permute-start(f32[32,1,16,128]{3,0,2,1:T(8,128)S(1)} %get-tuple-element.31), channel_id=1, source_target_pairs={{4,0},{8,4},{12,8},{16,12},{20,16},{24,20},{28,24},{0,28},{5,1},{9... | collective-permute-start | bytes 786440 | tf_op jit(solution)/shard_map/ppermute | solution.py:18
  125.5 4.5 %collective-permute-start.6 = (f32[32,4,1,128]{3,0,2,1:T(8,128)S(1)}, f32[32,4,1,128]{3,0,2,1:T(8,128)S(1)}, u32[]{:S(2)}, u32[]{:S(2)}) collective-permute-start(f32[32,4,1,128]{3,0,2,1:T(8,128)S(1)} %get-tuple-element.16), channel_id=1, source_target_pairs={{1,0},{2,1},{3,2},{0,3},{5,4},{6,5},{7,6},{4,7},{9,8},{10,9},{11,1... | collective-permute-start | bytes 196616 | tf_op jit(solution)/shard_map/ppermute | solution.py:18
  125.6 5.3 %collective-permute-start.7 = (f32[32,4,1,128]{3,0,2,1:T(8,128)S(1)}, f32[32,4,1,128]{3,0,2,1:T(8,128)S(1)}, u32[]{:S(2)}, u32[]{:S(2)}) collective-permute-start(f32[32,4,1,128]{3,0,2,1:T(8,128)S(1)} %get-tuple-element.17), channel_id=1, source_target_pairs={{0,1},{1,2},{2,3},{3,0},{4,5},{5,6},{6,7},{7,4},{8,9},{9,10},{10,1... | collective-permute-start | bytes 196616 | tf_op jit(solution)/shard_map/ppermute | solution.py:15
  184.4 6.8 %collective-permute-start.9 = (f32[32,1,16,128]{3,0,2,1:T(8,128)S(1)}, f32[32,1,16,128]{3,0,2,1:T(8,128)S(1)}, u32[]{:S(2)}, u32[]{:S(2)}) collective-permute-start(f32[32,1,16,128]{3,0,2,1:T(8,128)S(1)} %get-tuple-element.24), channel_id=1, source_target_pairs={{0,4},{4,8},{8,12},{12,16},{16,20},{20,24},{24,28},{28,0},{1,5},{5... | collective-permute-start | bytes 786440 | tf_op jit(solution)/shard_map/ppermute | solution.py:15
  184.4 6.8 %collective-permute-start.8 = (f32[32,1,16,128]{3,0,2,1:T(8,128)S(1)}, f32[32,1,16,128]{3,0,2,1:T(8,128)S(1)}, u32[]{:S(2)}, u32[]{:S(2)}) collective-permute-start(f32[32,1,16,128]{3,0,2,1:T(8,128)S(1)} %get-tuple-element.25), channel_id=1, source_target_pairs={{4,0},{8,4},{12,8},{16,12},{20,16},{24,20},{28,24},{0,28},{5,1},{9... | collective-permute-start | bytes 786440 | tf_op jit(solution)/shard_map/ppermute | solution.py:18
  191.2 4.3 %collective-permute-start.10 = (f32[32,4,1,128]{3,0,2,1:T(8,128)S(1)}, f32[32,4,1,128]{3,0,2,1:T(8,128)S(1)}, u32[]{:S(2)}, u32[]{:S(2)}) collective-permute-start(f32[32,4,1,128]{3,0,2,1:T(8,128)S(1)} %get-tuple-element.14), channel_id=1, source_target_pairs={{1,0},{2,1},{3,2},{0,3},{5,4},{6,5},{7,6},{4,7},{9,8},{10,9},{11,1... | collective-permute-start | bytes 196616 | tf_op jit(solution)/shard_map/ppermute | solution.py:18
  191.3 4.8 %collective-permute-start.11 = (f32[32,4,1,128]{3,0,2,1:T(8,128)S(1)}, f32[32,4,1,128]{3,0,2,1:T(8,128)S(1)}, u32[]{:S(2)}, u32[]{:S(2)}) collective-permute-start(f32[32,4,1,128]{3,0,2,1:T(8,128)S(1)} %get-tuple-element.15), channel_id=1, source_target_pairs={{0,1},{1,2},{2,3},{3,0},{4,5},{5,6},{6,7},{7,4},{8,9},{9,10},{10,1... | collective-permute-start | bytes 196616 | tf_op jit(solution)/shard_map/ppermute | solution.py:15
where the time goes:
time: 254 us
  blocking collectives  171 us (67%)
  other arithmetic  28.9 us (11%)
  waiting for transfers between devices  24.1 us (9%)
  matrix products  13.3 us (5%)
  starting transfers between devices  11.6 us (5%)
  local copies, waits for them, and re-layouts  3.44 us (1%)
    psum x3, blocking collectives, per_device(): lax.psum((inner_block(current, image), inner_block(image, image)), ('gx',...  131 us
    psum x1, blocking collectives, per_device(): probe_matrix = lax.psum(inner_block(probes, probes), ('gx', 'gy'))  40.3 us
    ppermute x6, waiting for transfers between devices, with_halo(): lax.ppermute(lax.slice_in_dim(block, block.shape[dim] - width, None, axis...  16.7 us
    another operation x12, other arithmetic, inverse_lower(): lower_factor = jnp.linalg.cholesky(gram_matrix)  14.4 us
    another operation x6, other arithmetic, inverse_lower(): lax.linalg.triangular_solve(lower_factor, identity_matrix, left_side=True...  11 us
    dot_general x9, matrix products, combine(): jnp.einsum('pxyz,pq->qxyz', vectors, matrix, precision=lax.Precision.HIGH...  7.62 us
    ppermute x6, waiting for transfers between devices, with_halo(): lax.ppermute(lax.slice_in_dim(block, 0, width, axis=dim), axis, backward)  7.37 us
    ppermute x6, starting transfers between devices, with_halo(): lax.ppermute(lax.slice_in_dim(block, 0, width, axis=dim), axis, backward)  5.89 us
  transfers between devices with their start and end apart: 12, of which 10 were waited for; matrix products, arithmetic and copies ran while one was open for 0% of the time, Pallas kernels for 0%

commit v1 on v0

--- a/solution.py
+++ b/solution.py
@@ -67,8 +67,13 @@
         image = stencil(current, diagonal)
         if previous is not None:
             image = image - combine(previous, coupling)
-        projected, image_gram = lax.psum(
-            (inner_block(current, image), inner_block(image, image)), ("gx", "gy")
+
+        def samples_rest(w_in):
+            v_now = lax.psum(lax.psum(w_in, "gy"), "gx")
+            return v_now
+
+        projected, image_gram = samples_rest(
+            (inner_block(current, image), inner_block(image, image))
         )
         remain = image - combine(current, projected)
         remain_gram = image_gram - small_product(projected.T, projected)

time: 254 us -> 253 us (level)
  the two profiles are of different devices: /device:TPU:14 before, /device:TPU:0 now
where the time goes in v1:
time: 253 us
  blocking collectives  158 us (62%)
  waiting for transfers between devices  33.4 us (13%)
  other arithmetic  28.9 us (11%)
  starting transfers between devices  14.5 us (6%)
  matrix products  13.3 us (5%)
  local copies, waits for them, and re-layouts  3.44 us (1%)
    psum x6, blocking collectives, samples_rest(): v_now = lax.psum(lax.psum(w_in, 'gy'), 'gx')  116 us
    psum x1, blocking collectives, per_device(): probe_matrix = lax.psum(inner_block(probes, probes), ('gx', 'gy'))  42.1 us
    ppermute x6, waiting for transfers between devices, with_halo(): lax.ppermute(lax.slice_in_dim(block, block.shape[dim] - width, None, axis...  26.4 us
    another operation x12, other arithmetic, inverse_lower(): lower_factor = jnp.linalg.cholesky(gram_matrix)  14.4 us
    ppermute x6, starting transfers between devices, with_halo(): lax.ppermute(lax.slice_in_dim(block, 0, width, axis=dim), axis, backward)  13.1 us
    another operation x6, other arithmetic, inverse_lower(): lax.linalg.triangular_solve(lower_factor, identity_matrix, left_side=True...  11 us
    dot_general x9, matrix products, combine(): jnp.einsum('pxyz,pq->qxyz', vectors, matrix, precision=lax.Precision.HIGH...  7.63 us
    ppermute x6, waiting for transfers between devices, with_halo(): lax.ppermute(lax.slice_in_dim(block, 0, width, axis=dim), axis, backward)  6.96 us
  transfers between devices with their start and end apart: 12, of which 10 were waited for; matrix products, arithmetic and copies ran while one was open for 0% of the time, Pallas kernels for 0%

profile of v1, /device:TPU:0, one launch (start us, length us, event | category | flops | bytes accessed | tf_op | source)
XLA Modules:
  0.0 252.7 jit_solution(17278032566777681876)
XLA Ops:
  2.6 42.1 %psum.91 = f32[32,32]{0,1:T(8,128)S(1)} all-reduce(f32[32,32]{0,1:T(8,128)S(1)} %convolution_bitcast_fusion.10), channel_id=1, replica_groups=mesh['gx'=8,'gy'=4] {'gx','gy'}, use_global_device_ids=true, to_apply=%region_0.0 | all-reduce | flops 1024 | bytes 8192 | tf_op jit(solution)/shard_map/psum | solution.py:59
  44.7 2.9 %cholesky.74 = f32[32,32]{1,0:T(8,128)S(1)} custom-call(f32[32,32]{1,0:T(8,128)S(1)} %fusion.38), custom_call_target="Cholesky" | custom-call | tf_op jit(solution)/shard_map/jit(cholesky)/cholesky | solution.py:43
  49.0 2.4 custom-call.8
  52.7 2.6 %collective-permute-start = (f32[32,1,16,128]{3,0,2,1:T(8,128)S(1)}, f32[32,1,16,128]{3,0,2,1:T(8,128)S(1)}, u32[]{:S(2)}, u32[]{:S(2)}) collective-permute-start(f32[32,1,16,128]{3,0,2,1:T(8,128)S(1)} %get-tuple-element.43), channel_id=1, source_target_pairs={{4,0},{8,4},{12,8},{16,12},{20,16},{24,20},{28,24},{0,28},{5,1},{9... | collective-permute-start | bytes 786440 | tf_op jit(solution)/shard_map/ppermute | solution.py:18
  55.7 4.8 %collective-permute-done.1 = f32[32,1,16,128]{3,0,2,1:T(8,128)S(1)} collective-permute-done((f32[32,1,16,128]{3,0,2,1:T(8,128)S(1)}, f32[32,1,16,128]{3,0,2,1:T(8,128)S(1)}, u32[]{:S(2)}, u32[]{:S(2)}) %collective-permute-start.1) | collective-permute-done | bytes 262176 | tf_op jit(solution)/shard_map/ppermute | solution.py:15
  61.1 2.3 collective-permute-start.2
  63.3 2.0 collective-permute-done.2
  65.4 4.2 %collective-permute-done.3 = f32[32,4,1,128]{3,0,2,1:T(8,128)S(1)} collective-permute-done((f32[32,4,1,128]{3,0,2,1:T(8,128)S(1)}, f32[32,4,1,128]{3,0,2,1:T(8,128)S(1)}, u32[]{:S(2)}, u32[]{:S(2)}) %collective-permute-start.3) | collective-permute-done | bytes 65568 | tf_op jit(solution)/shard_map/ppermute | solution.py:15
  71.1 17.1 %all-reduce.5 = (f32[32,32]{0,1:T(8,128)S(1)}, f32[32,32]{1,0:T(8,128)S(1)}) all-reduce(f32[32,32]{0,1:T(8,128)S(1)} %convolution_bitcast_fusion.7, f32[32,32]{1,0:T(8,128)S(1)} %convolution_bitcast_fusion.8), channel_id=1, replica_groups=mesh['gx'=8,'gy'=4] {'gy'}, use_global_device_ids=true, to_apply=%region_5.8 | all-reduce | flops 2048 | bytes 16384 | tf_op jit(solution)/shard_map/psum | solution.py:72
  88.2 22.4 %all-reduce.2 = (f32[32,32]{0,1:T(8,128)S(1)}, f32[32,32]{1,0:T(8,128)S(1)}) all-reduce(f32[32,32]{0,1:T(8,128)S(1)} %get-tuple-element.18, f32[32,32]{1,0:T(8,128)S(1)} %get-tuple-element.19), channel_id=1, replica_groups=mesh['gx'=8,'gy'=4] {'gx'}, use_global_device_ids=true, to_apply=%region_6.9 | all-reduce | flops 2048 | bytes 16384 | tf_op jit(solution)/shard_map/psum | solution.py:72
  111.5 2.9 %cholesky.85 = f32[32,32]{1,0:T(8,128)S(1)} custom-call(f32[32,32]{1,0:T(8,128)S(1)} %fusion.36), custom_call_target="Cholesky" | custom-call | tf_op jit(solution)/shard_map/jit(cholesky)/cholesky | solution.py:43
  115.8 2.4 custom-call.9
  119.2 2.6 %collective-permute-start.4 = (f32[32,1,16,128]{3,0,2,1:T(8,128)S(1)}, f32[32,1,16,128]{3,0,2,1:T(8,128)S(1)}, u32[]{:S(2)}, u32[]{:S(2)}) collective-permute-start(f32[32,1,16,128]{3,0,2,1:T(8,128)S(1)} %get-tuple-element.37), channel_id=1, source_target_pairs={{4,0},{8,4},{12,8},{16,12},{20,16},{24,20},{28,24},{0,28},{5,1},{9... | collective-permute-start | bytes 786440 | tf_op jit(solution)/shard_map/ppermute | solution.py:18
  122.0 5.8 %collective-permute-done.5 = f32[32,1,16,128]{3,0,2,1:T(8,128)S(1)} collective-permute-done((f32[32,1,16,128]{3,0,2,1:T(8,128)S(1)}, f32[32,1,16,128]{3,0,2,1:T(8,128)S(1)}, u32[]{:S(2)}, u32[]{:S(2)}) %collective-permute-start.5) | collective-permute-done | bytes 262176 | tf_op jit(solution)/shard_map/ppermute | solution.py:15
  127.8 1.3 collective-permute-start.6
  130.1 2.3 collective-permute-done.6
  132.5 2.8 %collective-permute-done.7 = f32[32,4,1,128]{3,0,2,1:T(8,128)S(1)} collective-permute-done((f32[32,4,1,128]{3,0,2,1:T(8,128)S(1)}, f32[32,4,1,128]{3,0,2,1:T(8,128)S(1)}, u32[]{:S(2)}, u32[]{:S(2)}) %collective-permute-start.7) | collective-permute-done | bytes 65568 | tf_op jit(solution)/shard_map/ppermute | solution.py:15
  135.2 1.6 convolution_subtract_fusion.3
  137.9 15.8 %all-reduce.4 = (f32[32,32]{0,1:T(8,128)S(1)}, f32[32,32]{1,0:T(8,128)S(1)}) all-reduce(f32[32,32]{0,1:T(8,128)S(1)} %convolution_bitcast_fusion.4, f32[32,32]{1,0:T(8,128)S(1)} %convolution_bitcast_fusion.5), channel_id=1, replica_groups=mesh['gx'=8,'gy'=4] {'gy'}, use_global_device_ids=true, to_apply=%region_9.12 | all-reduce | flops 2048 | bytes 16384 | tf_op jit(solution)/shard_map/psum | solution.py:72
  153.7 22.6 %all-reduce.1 = (f32[32,32]{0,1:T(8,128)S(1)}, f32[32,32]{1,0:T(8,128)S(1)}) all-reduce(f32[32,32]{0,1:T(8,128)S(1)} %get-tuple-element.16, f32[32,32]{1,0:T(8,128)S(1)} %get-tuple-element.17), channel_id=1, replica_groups=mesh['gx'=8,'gy'=4] {'gx'}, use_global_device_ids=true, to_apply=%region_10.13 | all-reduce | flops 2048 | bytes 16384 | tf_op jit(solution)/shard_map/psum | solution.py:72
  177.2 2.9 %cholesky.96 = f32[32,32]{1,0:T(8,128)S(1)} custom-call(f32[32,32]{1,0:T(8,128)S(1)} %fusion.33), custom_call_target="Cholesky" | custom-call | tf_op jit(solution)/shard_map/jit(cholesky)/cholesky | solution.py:43
  181.5 2.4 custom-call.10
  184.9 2.6 %collective-permute-start.8 = (f32[32,1,16,128]{3,0,2,1:T(8,128)S(1)}, f32[32,1,16,128]{3,0,2,1:T(8,128)S(1)}, u32[]{:S(2)}, u32[]{:S(2)}) collective-permute-start(f32[32,1,16,128]{3,0,2,1:T(8,128)S(1)} %get-tuple-element.31), channel_id=1, source_target_pairs={{4,0},{8,4},{12,8},{16,12},{20,16},{24,20},{28,24},{0,28},{5,1},{9... | collective-permute-start | bytes 786440 | tf_op jit(solution)/shard_map/ppermute | solution.py:18
  187.7 5.4 %collective-permute-done.9 = f32[32,1,16,128]{3,0,2,1:T(8,128)S(1)} collective-permute-done((f32[32,1,16,128]{3,0,2,1:T(8,128)S(1)}, f32[32,1,16,128]{3,0,2,1:T(8,128)S(1)}, u32[]{:S(2)}, u32[]{:S(2)}) %collective-permute-start.9) | collective-permute-done | bytes 262176 | tf_op jit(solution)/shard_map/ppermute | solution.py:15
  193.1 1.7 collective-permute-start.10
  195.4 2.0 collective-permute-done.10
  197.5 3.4 %collective-permute-done.11 = f32[32,4,1,128]{3,0,2,1:T(8,128)S(1)} collective-permute-done((f32[32,4,1,128]{3,0,2,1:T(8,128)S(1)}, f32[32,4,1,128]{3,0,2,1:T(8,128)S(1)}, u32[]{:S(2)}, u32[]{:S(2)}) %collective-permute-start.11) | collective-permute-done | bytes 65568 | tf_op jit(solution)/shard_map/ppermute | solution.py:15
  200.9 1.6 convolution_subtract_fusion.1
  203.6 15.8 %all-reduce.3 = (f32[32,32]{1,0:T(8,128)S(1)}, f32[32,32]{0,1:T(8,128)S(1)}) all-reduce(f32[32,32]{1,0:T(8,128)S(1)} %convolution_bitcast_fusion.2, f32[32,32]{0,1:T(8,128)S(1)} %convolution_bitcast_fusion.1), channel_id=1, replica_groups=mesh['gx'=8,'gy'=4] {'gy'}, use_global_device_ids=true, to_apply=%region_11.14 | all-reduce | flops 2048 | bytes 16384 | tf_op jit(solution)/shard_map/psum | solution.py:72
  219.4 22.4 %all-reduce = (f32[32,32]{1,0:T(8,128)S(1)}, f32[32,32]{0,1:T(8,128)S(1)}) all-reduce(f32[32,32]{1,0:T(8,128)S(1)} %get-tuple-element.14, f32[32,32]{0,1:T(8,128)S(1)} %get-tuple-element.15), channel_id=1, replica_groups=mesh['gx'=8,'gy'=4] {'gx'}, use_global_device_ids=true, to_apply=%region_12.15 | all-reduce | flops 2048 | bytes 16384 | tf_op jit(solution)/shard_map/psum | solution.py:72
  242.7 2.9 %cholesky.107 = f32[32,32]{1,0:T(8,128)S(1)} custom-call(f32[32,32]{1,0:T(8,128)S(1)} %fusion.30), custom_call_target="Cholesky" | custom-call | tf_op jit(solution)/shard_map/jit(cholesky)/cholesky | solution.py:43
  247.0 2.4 custom-call.11
  (71 shorter events, 23.0 us)
Async XLA Ops:
  52.6 7.9 %collective-permute-start.1 = (f32[32,1,16,128]{3,0,2,1:T(8,128)S(1)}, f32[32,1,16,128]{3,0,2,1:T(8,128)S(1)}, u32[]{:S(2)}, u32[]{:S(2)}) collective-permute-start(f32[32,1,16,128]{3,0,2,1:T(8,128)S(1)} %get-tuple-element.42), channel_id=1, source_target_pairs={{0,4},{4,8},{8,12},{12,16},{16,20},{20,24},{24,28},{28,0},{1,5},{5... | collective-permute-start | bytes 786440 | tf_op jit(solution)/shard_map/ppermute | solution.py:15
  52.7 8.4 %collective-permute-start = (f32[32,1,16,128]{3,0,2,1:T(8,128)S(1)}, f32[32,1,16,128]{3,0,2,1:T(8,128)S(1)}, u32[]{:S(2)}, u32[]{:S(2)}) collective-permute-start(f32[32,1,16,128]{3,0,2,1:T(8,128)S(1)} %get-tuple-element.43), channel_id=1, source_target_pairs={{4,0},{8,4},{12,8},{16,12},{20,16},{24,20},{28,24},{0,28},{5,1},{9... | collective-permute-start | bytes 786440 | tf_op jit(solution)/shard_map/ppermute | solution.py:18
  55.7 7.6 %copy-start = (f32[2,16,128]{2,1,0:T(8,128)S(1)}, f32[2,16,128]{2,1,0:T(8,128)}, u32[]{:S(2)}) copy-start(f32[2,16,128]{2,1,0:T(8,128)} %param.6) | copy-start | bytes 49156
  61.1 4.3 %collective-permute-start.2 = (f32[32,4,1,128]{3,0,2,1:T(8,128)S(1)}, f32[32,4,1,128]{3,0,2,1:T(8,128)S(1)}, u32[]{:S(2)}, u32[]{:S(2)}) collective-permute-start(f32[32,4,1,128]{3,0,2,1:T(8,128)S(1)} %get-tuple-element.24), channel_id=1, source_target_pairs={{1,0},{2,1},{3,2},{0,3},{5,4},{6,5},{7,6},{4,7},{9,8},{10,9},{11,1... | collective-permute-start | bytes 196616 | tf_op jit(solution)/shard_map/ppermute | solution.py:18
  63.3 6.2 %collective-permute-start.3 = (f32[32,4,1,128]{3,0,2,1:T(8,128)S(1)}, f32[32,4,1,128]{3,0,2,1:T(8,128)S(1)}, u32[]{:S(2)}, u32[]{:S(2)}) collective-permute-start(f32[32,4,1,128]{3,0,2,1:T(8,128)S(1)} %get-tuple-element.25), channel_id=1, source_target_pairs={{0,1},{1,2},{2,3},{3,0},{4,5},{5,6},{6,7},{7,4},{8,9},{9,10},{10,1... | collective-permute-start | bytes 196616 | tf_op jit(solution)/shard_map/ppermute | solution.py:15
  119.1 8.7 %collective-permute-start.5 = (f32[32,1,16,128]{3,0,2,1:T(8,128)S(1)}, f32[32,1,16,128]{3,0,2,1:T(8,128)S(1)}, u32[]{:S(2)}, u32[]{:S(2)}) collective-permute-start(f32[32,1,16,128]{3,0,2,1:T(8,128)S(1)} %get-tuple-element.36), channel_id=1, source_target_pairs={{0,4},{4,8},{8,12},{12,16},{16,20},{20,24},{24,28},{28,0},{1,5},{5... | collective-permute-start | bytes 786440 | tf_op jit(solution)/shard_map/ppermute | solution.py:15
  119.2 8.7 %collective-permute-start.4 = (f32[32,1,16,128]{3,0,2,1:T(8,128)S(1)}, f32[32,1,16,128]{3,0,2,1:T(8,128)S(1)}, u32[]{:S(2)}, u32[]{:S(2)}) collective-permute-start(f32[32,1,16,128]{3,0,2,1:T(8,128)S(1)} %get-tuple-element.37), channel_id=1, source_target_pairs={{4,0},{8,4},{12,8},{16,12},{20,16},{24,20},{28,24},{0,28},{5,1},{9... | collective-permute-start | bytes 786440 | tf_op jit(solution)/shard_map/ppermute | solution.py:18
  127.8 4.6 %collective-permute-start.6 = (f32[32,4,1,128]{3,0,2,1:T(8,128)S(1)}, f32[32,4,1,128]{3,0,2,1:T(8,128)S(1)}, u32[]{:S(2)}, u32[]{:S(2)}) collective-permute-start(f32[32,4,1,128]{3,0,2,1:T(8,128)S(1)} %get-tuple-element.22), channel_id=1, source_target_pairs={{1,0},{2,1},{3,2},{0,3},{5,4},{6,5},{7,6},{4,7},{9,8},{10,9},{11,1... | collective-permute-start | bytes 196616 | tf_op jit(solution)/shard_map/ppermute | solution.py:18
  129.2 6.1 %collective-permute-start.7 = (f32[32,4,1,128]{3,0,2,1:T(8,128)S(1)}, f32[32,4,1,128]{3,0,2,1:T(8,128)S(1)}, u32[]{:S(2)}, u32[]{:S(2)}) collective-permute-start(f32[32,4,1,128]{3,0,2,1:T(8,128)S(1)} %get-tuple-element.23), channel_id=1, source_target_pairs={{0,1},{1,2},{2,3},{3,0},{4,5},{5,6},{6,7},{7,4},{8,9},{9,10},{10,1... | collective-permute-start | bytes 196616 | tf_op jit(solution)/shard_map/ppermute | solution.py:15
  184.8 8.3 %collective-permute-start.9 = (f32[32,1,16,128]{3,0,2,1:T(8,128)S(1)}, f32[32,1,16,128]{3,0,2,1:T(8,128)S(1)}, u32[]{:S(2)}, u32[]{:S(2)}) collective-permute-start(f32[32,1,16,128]{3,0,2,1:T(8,128)S(1)} %get-tuple-element.30), channel_id=1, source_target_pairs={{0,4},{4,8},{8,12},{12,16},{16,20},{20,24},{24,28},{28,0},{1,5},{5... | collective-permute-start | bytes 786440 | tf_op jit(solution)/shard_map/ppermute | solution.py:15
  184.9 8.3 %collective-permute-start.8 = (f32[32,1,16,128]{3,0,2,1:T(8,128)S(1)}, f32[32,1,16,128]{3,0,2,1:T(8,128)S(1)}, u32[]{:S(2)}, u32[]{:S(2)}) collective-permute-start(f32[32,1,16,128]{3,0,2,1:T(8,128)S(1)} %get-tuple-element.31), channel_id=1, source_target_pairs={{4,0},{8,4},{12,8},{16,12},{20,16},{24,20},{28,24},{0,28},{5,1},{9... | collective-permute-start | bytes 786440 | tf_op jit(solution)/shard_map/ppermute | solution.py:18
  193.1 4.3 %collective-permute-start.10 = (f32[32,4,1,128]{3,0,2,1:T(8,128)S(1)}, f32[32,4,1,128]{3,0,2,1:T(8,128)S(1)}, u32[]{:S(2)}, u32[]{:S(2)}) collective-permute-start(f32[32,4,1,128]{3,0,2,1:T(8,128)S(1)} %get-tuple-element.20), channel_id=1, source_target_pairs={{1,0},{2,1},{3,2},{0,3},{5,4},{6,5},{7,6},{4,7},{9,8},{10,9},{11,1... | collective-permute-start | bytes 196616 | tf_op jit(solution)/shard_map/ppermute | solution.py:18
  194.8 6.1 %collective-permute-start.11 = (f32[32,4,1,128]{3,0,2,1:T(8,128)S(1)}, f32[32,4,1,128]{3,0,2,1:T(8,128)S(1)}, u32[]{:S(2)}, u32[]{:S(2)}) collective-permute-start(f32[32,4,1,128]{3,0,2,1:T(8,128)S(1)} %get-tuple-element.21), channel_id=1, source_target_pairs={{0,1},{1,2},{2,3},{3,0},{4,5},{5,6},{6,7},{7,4},{8,9},{9,10},{10,1... | collective-permute-start | bytes 196616 | tf_op jit(solution)/shard_map/ppermute | solution.py:15
